TPU v7x, 32 devices: a whole 2x2x4 slice. The times are simulated.
32 devices in a mesh: line: 2 (over y), bin: 16 (over z, x, core).
Axes of the slice: x: 2, y: 2, z: 4, core: 2. Of those that a mesh axis runs over, the one named last changes fastest.
Arguments:
- predicted: bfloat16 [4096, 2048], P(('line', 'bin')), parts along dimension 0, may hold values from -1200 to 1200
- observed: float32 [4096, 2048], P(('line', 'bin')), parts along dimension 0, may hold values from -1200 to 1200
- data_weight: float32 [4096, 2048], P(('line', 'bin')), parts along dimension 0, may hold values from 0.5 to 2
- bin_ids: int32 [4096], P(('line', 'bin')), parts along dimension 0, may hold values from 0 to 31, as said below
- offset_slots: int32 [4096], P(('line', 'bin')), parts along dimension 0, may hold values from 0 to 63, as said below
- conv_in: bfloat16 [3, 3, 48], replicated, may hold values from -2 to 2
- conv_mid: bfloat16 [3, 3, 48, 48], replicated, may hold values from -0.3125 to 0.3125
- conv_out: bfloat16 [3, 3, 48], replicated, may hold values from -0.3125 to 0.3125
Outputs:
- residual_traces: bfloat16 [4096, 2048], P(('line', 'bin')), parts along dimension 0
There are 2 independent parts, one for each index of `line`. A program takes and returns all parts, laid end to end along the dimension named above; an argument that names none is the same for every part. Nothing has to cross between parts.
Inputs may be any that keep to these rules, and one draw needn't show every extreme that they name: `bin_ids`: bin b belongs to index b // 2 of bin. The traces of one device go at most 16 to one owner and at most 8 to one bin, both reached in every draw. Taken by owner index minus the sender's index, modulo the devices of bin, every device sends the same counts. Every owner receives exactly 128 traces, 64 in each of its bins. `offset_slots`: no two traces have the same bin and slot.
All inputs are finite; a program needn't handle non-finite values.
Results may differ from a plain program's by a relative error of at most 0.0065.
Values may be sent and summed in bfloat16 or wider, within the bound.
A program may use at most 256 MiB of HBM per device.

v0:
```python
import jax
import jax.numpy as jnp
from jax import lax
from jax.sharding import PartitionSpec as P

OFFS = 64
rim_width = 6
window_span = 512
kept_span = 500


def shifted(values, along_offset, along_time):
    last = values.ndim - 1
    span_x = values.shape[-2]
    span_t = values.shape[-1]
    pad_x = abs(along_offset)
    pad_t = abs(along_time)
    widths = [(0, 0)] * (values.ndim - 2) + [(pad_x, pad_x), (pad_t, pad_t)]
    padded = jnp.pad(values, widths)
    padded = lax.slice_in_dim(
        padded, pad_x + along_offset, pad_x + along_offset + span_x, axis=last - 1
    )
    return lax.slice_in_dim(padded, pad_t + along_time, pad_t + along_time + span_t, axis=last)


def filter_panels(panels, conv_in, conv_mid, conv_out):
    bin_count, offsets, samples = panels.shape
    blocks = -(-samples // kept_span)
    extent = blocks * kept_span
    padded = jnp.pad(panels, ((0, 0), (0, 0), (rim_width, extent - samples + rim_width)))
    channels = conv_in.shape[-1]

    def one_block(block, result):
        start = block * kept_span
        window = lax.dynamic_slice_in_dim(padded, start, window_span, 2)
        times = start - rim_width + jnp.arange(window_span, dtype=jnp.int32)
        inside = (times >= 0) & (times < samples)
        values = window.astype(jnp.float32)
        first_sum = jnp.zeros((channels,) + values.shape, jnp.float32)
        for row_tap in range(3):
            for time_tap in range(3):
                weights = conv_in[row_tap, time_tap].astype(jnp.float32)
                first_sum = (
                    first_sum
                    + weights[:, None, None, None]
                    * shifted(values, row_tap - 1, time_tap - 1)[None]
                )
        first_hidden = jnp.where(inside, jax.nn.silu(first_sum), 0.0).astype(jnp.bfloat16)
        second_sum = jnp.zeros((channels,) + values.shape, jnp.float32)
        for row_tap in range(3):
            for time_tap in range(3):
                second_sum = second_sum + jnp.einsum(
                    "io,inxt->onxt",
                    conv_mid[row_tap, time_tap],
                    shifted(first_hidden, 2 * (row_tap - 1), 4 * (time_tap - 1)),
                    preferred_element_type=jnp.float32,
                )
        second_hidden = jnp.where(
            inside, first_hidden.astype(jnp.float32) + jax.nn.silu(second_sum), 0.0
        ).astype(jnp.bfloat16)
        third_sum = jnp.zeros(values.shape, jnp.float32)
        for row_tap in range(3):
            for time_tap in range(3):
                third_sum = third_sum + jnp.einsum(
                    "i,inxt->nxt",
                    conv_out[row_tap, time_tap],
                    shifted(second_hidden, row_tap - 1, time_tap - 1),
                    preferred_element_type=jnp.float32,
                )
        output = (values + third_sum).astype(jnp.bfloat16)
        piece = output[:, :, rim_width : rim_width + kept_span]
        return lax.dynamic_update_slice_in_dim(result, piece, start, 2)

    result = jnp.zeros((bin_count, offsets, extent), jnp.bfloat16)
    result = lax.fori_loop(0, blocks, one_block, result)
    return result[:, :, :samples]


def local(predicted, observed, data_weight, bin_ids, offset_slots, conv_in, conv_mid, conv_out):
    tr_dev, samples = predicted.shape
    owners = lax.axis_size("bin")
    bin_dev = tr_dev // OFFS
    capacity = max(bin_dev, 2 * tr_dev // owners)
    owner_dev = bin_ids // bin_dev
    local_bin = bin_ids % bin_dev
    row_index = jnp.arange(tr_dev, dtype=jnp.int32)
    earlier = row_index[None, :] < row_index[:, None]
    same_owner = owner_dev[:, None] == owner_dev[None, :]
    position = jnp.sum((same_owner & earlier).astype(jnp.int32), axis=1)
    send_slot = owner_dev * capacity + position
    panel_cell = local_bin * OFFS + offset_slots
    outgoing = (
        jnp.zeros((owners * capacity, samples), jnp.bfloat16)
        .at[send_slot]
        .set(predicted)
        .reshape(owners, capacity, samples)
    )
    outgoing_cells = (
        jnp.full((owners * capacity,), -1, jnp.int32)
        .at[send_slot]
        .set(panel_cell)
        .reshape(owners, capacity)
    )
    arrived, arrived_cells = (
        lax.all_to_all(outgoing, "bin", split_axis=0, concat_axis=0, tiled=True),
        lax.all_to_all(outgoing_cells, "bin", split_axis=0, concat_axis=0, tiled=True),
    )
    flat_cells = arrived_cells.reshape(-1)
    filled = flat_cells >= 0
    target = jnp.where(filled, flat_cells, bin_dev * OFFS)
    panels = (
        jnp.zeros((bin_dev * OFFS, samples), jnp.bfloat16)
        .at[target]
        .set(arrived.reshape(-1, samples), mode="drop")
        .reshape(bin_dev, OFFS, samples)
    )
    filtered = filter_panels(panels, conv_in, conv_mid, conv_out).reshape(bin_dev * OFFS, samples)
    answer = jnp.where(
        filled[:, None], filtered[jnp.where(filled, flat_cells, 0)], jnp.zeros((), jnp.bfloat16)
    ).reshape(owners, capacity, samples)
    returned = lax.all_to_all(answer, "bin", split_axis=0, concat_axis=0, tiled=True)
    own_rows = returned.reshape(-1, samples)[send_slot]
    misfit = data_weight * (own_rows.astype(jnp.float32) - observed)
    misfit_total = lax.psum(jnp.sum(misfit * misfit), "bin")
    mean_square = misfit_total / (tr_dev * owners * samples)
    return (misfit * lax.rsqrt(mean_square + 1e-05)).astype(jnp.bfloat16)


def solution(mesh):
    in_specs = (
        P(("line", "bin"), None),
        P(("line", "bin"), None),
        P(("line", "bin"), None),
        P(("line", "bin")),
        P(("line", "bin")),
        P(),
        P(),
        P(),
    )
    out_specs = P(("line", "bin"), None)
    return jax.shard_map(local, mesh=mesh, in_specs=in_specs, out_specs=out_specs, check_vma=False)
```

profile of v0, /device:TPU:0, one launch (start us, length us, event | category | flops | bytes accessed | tf_op | source)
XLA Modules:
  0.0 748.5 jit_solution(1214765087645335547)
XLA Ops:
  2.6 7.4 all-to-all-start
  23.4 19.4 %all-to-all-done.1 = bf16[16,16,2048]{2,1,0:T(8,128)(2,1)S(1)} async-done(((bf16[16,16,2048]{2,1,0:T(8,128)(2,1)}), bf16[16,16,2048]{2,1,0:T(8,128)(2,1)S(1)}, u32[]{:S(2)}, u32[]{:S(2)}) %all-to-all-start.1) | async-done | bytes 1048608 | tf_op jit(solution)/shard_map/all_to_all | solution.py:105
  47.0 626.1 %while.15 = (s32[]{:T(128)}, bf16[2,64,2500]{2,1,0:T(8,128)(2,1)}, bf16[2,64,2512]{2,1,0:T(8,128)(2,1)}, bf16[3,3,48]{2,1,0:T(4,128)(2,1)}, bf16[3,3,48,48]{2,3,...) while((s32[]{:T(128)}, bf16[2,64,2500]{2,1,0:T(8,128)(2,1)}, ...), condition=%wide.region_5.6_spmd, body=%wide.region_4.5_spmd.sunk | while | flops 3042436608 | bytes 363944288 | solution.py:75
  73.0 10.1 %select_convert_fusion.5 = bf16[48,2,64,512]{3,0,2,1:T(8,128)(2,1)S(1)} fusion(f32[2,64,512]{2,1,0:T(8,128)S(1)} %get-tuple-element.287, f32[48]{0:T(128)S(1)} %get-tuple-element.288, f32[2,64,512]{2,1,0:T(8,128)S(1)} %get-tuple-element.289, f32[48]{0:T(128)S(1)} %get-tuple-element.290, f32[2,64,512]{2,1,0:T(8,128)S(1)} %get-tuple-element.291, ...), kind=kLoop, calls=%fused_computation.12.clone.3 | loop fusion | flops 72351744 | bytes 8652992 | tf_op jit(solution)/shard_map/while/body/eval_jaxpr/convert_element_type | solution.py:48
  110.8 5.6 fusion.162
  122.0 5.6 fusion.160
  127.6 39.4 %fusion.168 = bf16[48,2,64,512]{3,0,2,1:T(8,128)(2,1)} fusion(f32[2,64,512,48]{2,3,1,0:T(8,128)} %fusion.160, f32[2,64,512,48]{2,3,1,0:T(8,128)} %fusion.161, f32[2,64,512,48]{2,3,1,0:T(8,128)} %fusion.162, f32[2,64,512,48]{2,3,1,0:T(8,128)} %fusion.163, f32[2,64,512,48]{2,3,1,0:T(8,128)} %fusion.164, f32[2,64,512,48]{2,3,1,0:T(8,128)} %fusion.165, ...), kind=kOutput, calls=%fused_computation.13.clone.1 | convolution fusion | flops 497025024 | bytes 111695872 | tf_op jit(solution)/shard_map/while/body/eval_jaxpr/io,inxt->onxt/dot_general | solution.py:52
  193.1 10.1 %select_convert_fusion.5 = bf16[48,2,64,512]{3,0,2,1:T(8,128)(2,1)S(1)} fusion(f32[2,64,512]{2,1,0:T(8,128)S(1)} %get-tuple-element.287, f32[48]{0:T(128)S(1)} %get-tuple-element.288, f32[2,64,512]{2,1,0:T(8,128)S(1)} %get-tuple-element.289, f32[48]{0:T(128)S(1)} %get-tuple-element.290, f32[2,64,512]{2,1,0:T(8,128)S(1)} %get-tuple-element.291, ...), kind=kLoop, calls=%fused_computation.12.clone.3 | loop fusion | flops 72351744 | bytes 8652992 | tf_op jit(solution)/shard_map/while/body/eval_jaxpr/convert_element_type | solution.py:48
  230.9 5.6 fusion.162
  242.1 5.6 fusion.160
  247.7 39.4 %fusion.168 = bf16[48,2,64,512]{3,0,2,1:T(8,128)(2,1)} fusion(f32[2,64,512,48]{2,3,1,0:T(8,128)} %fusion.160, f32[2,64,512,48]{2,3,1,0:T(8,128)} %fusion.161, f32[2,64,512,48]{2,3,1,0:T(8,128)} %fusion.162, f32[2,64,512,48]{2,3,1,0:T(8,128)} %fusion.163, f32[2,64,512,48]{2,3,1,0:T(8,128)} %fusion.164, f32[2,64,512,48]{2,3,1,0:T(8,128)} %fusion.165, ...), kind=kOutput, calls=%fused_computation.13.clone.1 | convolution fusion | flops 497025024 | bytes 111695872 | tf_op jit(solution)/shard_map/while/body/eval_jaxpr/io,inxt->onxt/dot_general | solution.py:52
  313.7 10.1 %select_convert_fusion.5 = bf16[48,2,64,512]{3,0,2,1:T(8,128)(2,1)S(1)} fusion(f32[2,64,512]{2,1,0:T(8,128)S(1)} %get-tuple-element.287, f32[48]{0:T(128)S(1)} %get-tuple-element.288, f32[2,64,512]{2,1,0:T(8,128)S(1)} %get-tuple-element.289, f32[48]{0:T(128)S(1)} %get-tuple-element.290, f32[2,64,512]{2,1,0:T(8,128)S(1)} %get-tuple-element.291, ...), kind=kLoop, calls=%fused_computation.12.clone.3 | loop fusion | flops 72351744 | bytes 8652992 | tf_op jit(solution)/shard_map/while/body/eval_jaxpr/convert_element_type | solution.py:48
  351.5 5.6 fusion.162
  362.7 5.6 fusion.160
  368.3 39.4 %fusion.168 = bf16[48,2,64,512]{3,0,2,1:T(8,128)(2,1)} fusion(f32[2,64,512,48]{2,3,1,0:T(8,128)} %fusion.160, f32[2,64,512,48]{2,3,1,0:T(8,128)} %fusion.161, f32[2,64,512,48]{2,3,1,0:T(8,128)} %fusion.162, f32[2,64,512,48]{2,3,1,0:T(8,128)} %fusion.163, f32[2,64,512,48]{2,3,1,0:T(8,128)} %fusion.164, f32[2,64,512,48]{2,3,1,0:T(8,128)} %fusion.165, ...), kind=kOutput, calls=%fused_computation.13.clone.1 | convolution fusion | flops 497025024 | bytes 111695872 | tf_op jit(solution)/shard_map/while/body/eval_jaxpr/io,inxt->onxt/dot_general | solution.py:52
  434.3 10.1 %select_convert_fusion.5 = bf16[48,2,64,512]{3,0,2,1:T(8,128)(2,1)S(1)} fusion(f32[2,64,512]{2,1,0:T(8,128)S(1)} %get-tuple-element.287, f32[48]{0:T(128)S(1)} %get-tuple-element.288, f32[2,64,512]{2,1,0:T(8,128)S(1)} %get-tuple-element.289, f32[48]{0:T(128)S(1)} %get-tuple-element.290, f32[2,64,512]{2,1,0:T(8,128)S(1)} %get-tuple-element.291, ...), kind=kLoop, calls=%fused_computation.12.clone.3 | loop fusion | flops 72351744 | bytes 8652992 | tf_op jit(solution)/shard_map/while/body/eval_jaxpr/convert_element_type | solution.py:48
  472.1 5.6 fusion.162
  488.9 39.4 %fusion.168 = bf16[48,2,64,512]{3,0,2,1:T(8,128)(2,1)} fusion(f32[2,64,512,48]{2,3,1,0:T(8,128)} %fusion.160, f32[2,64,512,48]{2,3,1,0:T(8,128)} %fusion.161, f32[2,64,512,48]{2,3,1,0:T(8,128)} %fusion.162, f32[2,64,512,48]{2,3,1,0:T(8,128)} %fusion.163, f32[2,64,512,48]{2,3,1,0:T(8,128)} %fusion.164, f32[2,64,512,48]{2,3,1,0:T(8,128)} %fusion.165, ...), kind=kOutput, calls=%fused_computation.13.clone.1 | convolution fusion | flops 497025024 | bytes 111695872 | tf_op jit(solution)/shard_map/while/body/eval_jaxpr/io,inxt->onxt/dot_general | solution.py:52
  554.9 10.1 %select_convert_fusion.5 = bf16[48,2,64,512]{3,0,2,1:T(8,128)(2,1)S(1)} fusion(f32[2,64,512]{2,1,0:T(8,128)S(1)} %get-tuple-element.287, f32[48]{0:T(128)S(1)} %get-tuple-element.288, f32[2,64,512]{2,1,0:T(8,128)S(1)} %get-tuple-element.289, f32[48]{0:T(128)S(1)} %get-tuple-element.290, f32[2,64,512]{2,1,0:T(8,128)S(1)} %get-tuple-element.291, ...), kind=kLoop, calls=%fused_computation.12.clone.3 | loop fusion | flops 72351744 | bytes 8652992 | tf_op jit(solution)/shard_map/while/body/eval_jaxpr/convert_element_type | solution.py:48
  592.7 5.6 fusion.162
  609.5 39.4 %fusion.168 = bf16[48,2,64,512]{3,0,2,1:T(8,128)(2,1)} fusion(f32[2,64,512,48]{2,3,1,0:T(8,128)} %fusion.160, f32[2,64,512,48]{2,3,1,0:T(8,128)} %fusion.161, f32[2,64,512,48]{2,3,1,0:T(8,128)} %fusion.162, f32[2,64,512,48]{2,3,1,0:T(8,128)} %fusion.163, f32[2,64,512,48]{2,3,1,0:T(8,128)} %fusion.164, f32[2,64,512,48]{2,3,1,0:T(8,128)} %fusion.165, ...), kind=kOutput, calls=%fused_computation.13.clone.1 | convolution fusion | flops 497025024 | bytes 111695872 | tf_op jit(solution)/shard_map/while/body/eval_jaxpr/io,inxt->onxt/dot_general | solution.py:52
  676.9 6.8 all-to-all-start.2
  683.7 22.9 %all-to-all-done.2 = bf16[16,16,2048]{2,1,0:T(8,128)(2,1)S(1)} async-done(((bf16[16,16,2048]{2,1,0:T(8,128)(2,1)}), bf16[16,16,2048]{2,1,0:T(8,128)(2,1)S(1)}, u32[]{:S(2)}, u32[]{:S(2)}) %all-to-all-start.2) | async-done | bytes 1048608 | tf_op jit(solution)/shard_map/all_to_all | solution.py:121
  709.7 35.5 %psum.7 = f32[]{:T(128)} all-reduce(f32[]{:T(128)} %multiply_reduce_fusion), channel_id=1, replica_groups=mesh['line'=2,'bin'=16] {'bin'}, use_global_device_ids=true, to_apply=%region_7.8 | all-reduce | flops 1 | bytes 8 | tf_op jit(solution)/shard_map/psum | solution.py:124
  (175 shorter events, 338.6 us)
Async XLA Ops:
  0.9 20.1 %copy-start.4 = (s32[128]{0:T(128)}, s32[128]{0:T(128)S(1)}, u32[]{:S(2)}) copy-start(s32[128]{0:T(128)S(1)} %compare_select_fusion.4) | copy-start | bytes 1540
  2.6 13.7 %all-to-all-start = ((s32[16,1,16]{2,1,0:T(1,128)}), s32[16,1,16]{2,1,0:T(1,128)S(1)}, u32[]{:S(2)}, u32[]{:S(2)}) async-start(s32[16,1,16]{2,1,0:T(1,128)} %all_to_all.12), calls=%async_computation | async-start | bytes 16384 | tf_op jit(solution)/shard_map/all_to_all | solution.py:106
  16.3 26.6 %all-to-all-start.1 = ((bf16[16,16,2048]{2,1,0:T(8,128)(2,1)}), bf16[16,16,2048]{2,1,0:T(8,128)(2,1)S(1)}, u32[]{:S(2)}, u32[]{:S(2)}) async-start(bf16[16,16,2048]{2,1,0:T(8,128)(2,1)} %bitcast.76), calls=%async_computation.1 | async-start | bytes 2097152 | tf_op jit(solution)/shard_map/all_to_all | solution.py:105
  47.0 628.8 %copy-start.3 = (pred[16,16]{1,0:T(8,128)(4,1)S(1)}, pred[16,16]{1,0:T(8,128)(4,1)}, u32[]{:S(2)}) copy-start(pred[16,16]{1,0:T(8,128)(4,1)} %compare_bitcast_fusion) | copy-start | bytes 772
  127.6 39.5 %copy-start.2 = (bf16[3,3,48]{2,1,0:T(4,128)(2,1)S(1)}, bf16[3,3,48]{2,1,0:T(4,128)(2,1)}, u32[]{:S(2)}) copy-start(bf16[3,3,48]{2,1,0:T(4,128)(2,1)} %get-tuple-element.337) | copy-start | bytes 2596 | tf_op jit(solution)/shard_map/while
  167.0 8.8 %copy-start = (bf16[48,2,64,512]{3,0,2,1:T(8,128)(2,1)S(1)}, bf16[48,2,64,512]{3,0,2,1:T(8,128)(2,1)}, u32[]{:S(2)}) copy-start(bf16[48,2,64,512]{3,0,2,1:T(8,128)(2,1)} %fusion.168) | copy-start | bytes 18874372 | tf_op jit(solution)/shard_map/while
  247.7 39.5 %copy-start.2 = (bf16[3,3,48]{2,1,0:T(4,128)(2,1)S(1)}, bf16[3,3,48]{2,1,0:T(4,128)(2,1)}, u32[]{:S(2)}) copy-start(bf16[3,3,48]{2,1,0:T(4,128)(2,1)} %get-tuple-element.337) | copy-start | bytes 2596 | tf_op jit(solution)/shard_map/while
  287.2 8.8 %copy-start = (bf16[48,2,64,512]{3,0,2,1:T(8,128)(2,1)S(1)}, bf16[48,2,64,512]{3,0,2,1:T(8,128)(2,1)}, u32[]{:S(2)}) copy-start(bf16[48,2,64,512]{3,0,2,1:T(8,128)(2,1)} %fusion.168) | copy-start | bytes 18874372 | tf_op jit(solution)/shard_map/while
  368.3 39.5 %copy-start.2 = (bf16[3,3,48]{2,1,0:T(4,128)(2,1)S(1)}, bf16[3,3,48]{2,1,0:T(4,128)(2,1)}, u32[]{:S(2)}) copy-start(bf16[3,3,48]{2,1,0:T(4,128)(2,1)} %get-tuple-element.337) | copy-start | bytes 2596 | tf_op jit(solution)/shard_map/while
  407.8 8.8 %copy-start = (bf16[48,2,64,512]{3,0,2,1:T(8,128)(2,1)S(1)}, bf16[48,2,64,512]{3,0,2,1:T(8,128)(2,1)}, u32[]{:S(2)}) copy-start(bf16[48,2,64,512]{3,0,2,1:T(8,128)(2,1)} %fusion.168) | copy-start | bytes 18874372 | tf_op jit(solution)/shard_map/while
  488.9 39.5 %copy-start.2 = (bf16[3,3,48]{2,1,0:T(4,128)(2,1)S(1)}, bf16[3,3,48]{2,1,0:T(4,128)(2,1)}, u32[]{:S(2)}) copy-start(bf16[3,3,48]{2,1,0:T(4,128)(2,1)} %get-tuple-element.337) | copy-start | bytes 2596 | tf_op jit(solution)/shard_map/while
  528.4 8.8 %copy-start = (bf16[48,2,64,512]{3,0,2,1:T(8,128)(2,1)S(1)}, bf16[48,2,64,512]{3,0,2,1:T(8,128)(2,1)}, u32[]{:S(2)}) copy-start(bf16[48,2,64,512]{3,0,2,1:T(8,128)(2,1)} %fusion.168) | copy-start | bytes 18874372 | tf_op jit(solution)/shard_map/while
  609.5 39.4 %copy-start.2 = (bf16[3,3,48]{2,1,0:T(4,128)(2,1)S(1)}, bf16[3,3,48]{2,1,0:T(4,128)(2,1)}, u32[]{:S(2)}) copy-start(bf16[3,3,48]{2,1,0:T(4,128)(2,1)} %get-tuple-element.337) | copy-start | bytes 2596 | tf_op jit(solution)/shard_map/while
  649.0 8.8 %copy-start = (bf16[48,2,64,512]{3,0,2,1:T(8,128)(2,1)S(1)}, bf16[48,2,64,512]{3,0,2,1:T(8,128)(2,1)}, u32[]{:S(2)}) copy-start(bf16[48,2,64,512]{3,0,2,1:T(8,128)(2,1)} %fusion.168) | copy-start | bytes 18874372 | tf_op jit(solution)/shard_map/while
  673.1 10.6 %copy-start.5 = (s32[128]{0:T(128)S(1)}, s32[128]{0:T(128)}, u32[]{:S(2)}) copy-start(s32[128]{0:T(128)} %copy-done.4) | copy-start | bytes 1540
  673.1 34.5 %copy-start.1 = (f32[128,2048]{1,0:T(8,128)S(1)}, f32[128,2048]{1,0:T(8,128)}, u32[]{:S(2)}) copy-start(f32[128,2048]{1,0:T(8,128)} %param.12) | copy-start | bytes 3145732
  676.9 29.8 %all-to-all-start.2 = ((bf16[16,16,2048]{2,1,0:T(8,128)(2,1)}), bf16[16,16,2048]{2,1,0:T(8,128)(2,1)S(1)}, u32[]{:S(2)}, u32[]{:S(2)}) async-start(bf16[16,16,2048]{2,1,0:T(8,128)(2,1)} %broadcast_select_fusion), calls=%async_computation.2 | async-start | bytes 2097152 | tf_op jit(solution)/shard_map/all_to_all | solution.py:121
where the time goes:
time: 753 us; the launch traced here: 748 us
  matrix products  526 us (70%)
  other arithmetic  71 us (9%)
  waiting for transfers between devices  45.7 us (6%)
  blocking collectives  35.5 us (5%)
  local copies, waits for them, and re-layouts  27.4 us (4%)
  loops' own time  24 us (3%)
  starting transfers between devices  17.8 us (2%)
    dot_general x45, matrix products, one_block(): jnp.einsum('io,inxt->onxt', conv_mid[row_tap, time_tap], shifted(first_hi...  420 us
    dot_general x45, matrix products, one_block(): jnp.einsum('i,inxt->nxt', conv_out[row_tap, time_tap], shifted(second_hid...  106 us
    convert_element_type x5, other arithmetic, one_block(): jnp.where(inside, jax.nn.silu(first_sum), 0.0).astype(jnp.bfloat16)  50.5 us
    psum x1, blocking collectives, local(): misfit_total = lax.psum(jnp.sum(misfit * misfit), 'bin')  35.5 us
    another operation x1, loops' own time, filter_panels(): result = lax.fori_loop(0, blocks, one_block, result)  24 us
    all_to_all x1, waiting for transfers between devices, local(): lax.all_to_all(answer, 'bin', split_axis=0, concat_axis=0, tiled=True)  22.9 us
    all_to_all x1, waiting for transfers between devices, local(): lax.all_to_all(outgoing, 'bin', split_axis=0, concat_axis=0, tiled=True)  19.4 us
  transfers between devices with their start and end apart: 3, of which 3 were waited for; matrix products, arithmetic and copies ran while one was open for 1% of the time, Pallas kernels for 0%

commit v1 on v0

--- a/solution.py
+++ b/solution.py
@@ -118,7 +118,15 @@
     answer = jnp.where(
         filled[:, None], filtered[jnp.where(filled, flat_cells, 0)], jnp.zeros((), jnp.bfloat16)
     ).reshape(owners, capacity, samples)
-    returned = lax.all_to_all(answer, "bin", split_axis=0, concat_axis=0, tiled=True)
+    ways, here = (lax.axis_size("bin"), lax.axis_index("bin"))
+    width = answer.shape[0] // ways
+    turned = jnp.roll(answer, -here * width, axis=0)
+    got = [lax.slice_in_dim(turned, 0, width, axis=0)]
+    for far in range(1, ways):
+        sent = lax.slice_in_dim(turned, far * width, (far + 1) * width, axis=0)
+        got.append(lax.ppermute(sent, "bin", [(d, (d + far) % ways) for d in range(ways)]))
+    line = jnp.concatenate(got[::-1], axis=0)
+    returned = jnp.roll(line, (here + 1) * got[0].shape[0], axis=0)
     own_rows = returned.reshape(-1, samples)[send_slot]
     misfit = data_weight * (own_rows.astype(jnp.float32) - observed)
     misfit_total = lax.psum(jnp.sum(misfit * misfit), "bin")

time: 753 us -> 786 us (1.044)
  starting transfers between devices: 17.8 us -> 53.6 us
    ppermute x0 -> x15, starting transfers between devices: none -> 42.6 us  [local(): lax.ppermute(sent, 'bin', [(d, (d + far) % ways) for d in range(ways)])]
    all_to_all x1 -> x0, waiting for transfers between devices: 22.9 us -> none  [local(): lax.all_to_all(answer, 'bin', split_axis=0, concat_axis=0, tiled=True)]
    ppermute x0 -> x15, waiting for transfers between devices: none -> 21.3 us  [local(): lax.ppermute(sent, 'bin', [(d, (d + far) % ways) for d in range(ways)])]
  transfers between devices with their start and end apart: 3 -> 17, of which waited for: 3 -> 12; matrix products, arithmetic and copies ran while one was open for 1% -> 1% of each run, Pallas kernels for 0% -> 0%
where the time goes in v1:
time: 786 us; the launch traced here: 781 us
  matrix products  525 us (67%)
  other arithmetic  70.8 us (9%)
  starting transfers between devices  53.6 us (7%)
  waiting for transfers between devices  44 us (6%)
  blocking collectives  32.3 us (4%)
  local copies, waits for them, and re-layouts  27.5 us (3%)
  loops' own time  26.4 us (3%)
    dot_general x45, matrix products, one_block(): jnp.einsum('io,inxt->onxt', conv_mid[row_tap, time_tap], shifted(first_hi...  419 us
    dot_general x45, matrix products, one_block(): jnp.einsum('i,inxt->nxt', conv_out[row_tap, time_tap], shifted(second_hid...  106 us
    convert_element_type x5, other arithmetic, one_block(): jnp.where(inside, jax.nn.silu(first_sum), 0.0).astype(jnp.bfloat16)  50.5 us
    ppermute x15, starting transfers between devices, local(): lax.ppermute(sent, 'bin', [(d, (d + far) % ways) for d in range(ways)])  42.6 us
    psum x1, blocking collectives, local(): misfit_total = lax.psum(jnp.sum(misfit * misfit), 'bin')  32.3 us
    another operation x1, loops' own time, filter_panels(): result = lax.fori_loop(0, blocks, one_block, result)  26.4 us
    ppermute x15, waiting for transfers between devices, local(): lax.ppermute(sent, 'bin', [(d, (d + far) % ways) for d in range(ways)])  21.3 us
    all_to_all x1, waiting for transfers between devices, local(): lax.all_to_all(outgoing, 'bin', split_axis=0, concat_axis=0, tiled=True)  19.3 us
  transfers between devices with their start and end apart: 17, of which 12 were waited for; matrix products, arithmetic and copies ran while one was open for 1% of the time, Pallas kernels for 0%

profile of v1, /device:TPU:0, one launch (start us, length us, event | category | flops | bytes accessed | tf_op | source)
XLA Modules:
  0.0 781.3 jit_solution(7336313192996342784)
XLA Ops:
  2.6 7.4 all-to-all-start
  23.5 19.3 %all-to-all-done.1 = bf16[16,16,2048]{2,1,0:T(8,128)(2,1)S(1)} async-done(((bf16[16,16,2048]{2,1,0:T(8,128)(2,1)}), bf16[16,16,2048]{2,1,0:T(8,128)(2,1)S(1)}, u32[]{:S(2)}, u32[]{:S(2)}) %all-to-all-start.1) | async-done | bytes 1048608 | tf_op jit(solution)/shard_map/all_to_all | solution.py:105
  46.9 628.1 %while.15 = (s32[]{:T(128)}, bf16[2,64,2500]{2,1,0:T(8,128)(2,1)}, bf16[2,64,2512]{2,1,0:T(8,128)(2,1)}, bf16[3,3,48]{2,1,0:T(4,128)(2,1)}, bf16[3,3,48,48]{2,3,...) while((s32[]{:T(128)}, bf16[2,64,2500]{2,1,0:T(8,128)(2,1)}, ...), condition=%wide.region_5.6_spmd, body=%wide.region_4.5_spmd.sunk | while | flops 3042436608 | bytes 363944288 | solution.py:75
  71.5 10.1 %select_convert_fusion.5 = bf16[48,2,64,512]{3,0,2,1:T(8,128)(2,1)S(1)} fusion(f32[2,64,512]{2,1,0:T(8,128)S(1)} %get-tuple-element.303, f32[48]{0:T(128)S(1)} %get-tuple-element.304, f32[2,64,512]{2,1,0:T(8,128)S(1)} %get-tuple-element.305, f32[48]{0:T(128)S(1)} %get-tuple-element.306, f32[2,64,512]{2,1,0:T(8,128)S(1)} %get-tuple-element.307, ...), kind=kLoop, calls=%fused_computation.12.clone.3 | loop fusion | flops 72351744 | bytes 8652992 | tf_op jit(solution)/shard_map/while/body/eval_jaxpr/convert_element_type | solution.py:48
  87.2 5.6 fusion.169
  109.3 5.6 fusion.165
  120.5 5.6 fusion.163
  126.1 39.3 %fusion.171 = bf16[48,2,64,512]{3,0,2,1:T(8,128)(2,1)} fusion(f32[2,64,512,48]{2,3,1,0:T(8,128)} %fusion.163, f32[2,64,512,48]{2,3,1,0:T(8,128)} %fusion.164, f32[2,64,512,48]{2,3,1,0:T(8,128)} %fusion.165, f32[2,64,512,48]{2,3,1,0:T(8,128)} %fusion.166, f32[2,64,512,48]{2,3,1,0:T(8,128)} %fusion.167, f32[2,64,512,48]{2,3,1,0:T(8,128)} %fusion.168, ...), kind=kOutput, calls=%fused_computation.13.clone.1 | convolution fusion | flops 497025024 | bytes 111695872 | tf_op jit(solution)/shard_map/while/body/eval_jaxpr/io,inxt->onxt/dot_general | solution.py:52
  191.6 10.1 %select_convert_fusion.5 = bf16[48,2,64,512]{3,0,2,1:T(8,128)(2,1)S(1)} fusion(f32[2,64,512]{2,1,0:T(8,128)S(1)} %get-tuple-element.303, f32[48]{0:T(128)S(1)} %get-tuple-element.304, f32[2,64,512]{2,1,0:T(8,128)S(1)} %get-tuple-element.305, f32[48]{0:T(128)S(1)} %get-tuple-element.306, f32[2,64,512]{2,1,0:T(8,128)S(1)} %get-tuple-element.307, ...), kind=kLoop, calls=%fused_computation.12.clone.3 | loop fusion | flops 72351744 | bytes 8652992 | tf_op jit(solution)/shard_map/while/body/eval_jaxpr/convert_element_type | solution.py:48
  229.4 5.6 fusion.165
  246.2 39.3 %fusion.171 = bf16[48,2,64,512]{3,0,2,1:T(8,128)(2,1)} fusion(f32[2,64,512,48]{2,3,1,0:T(8,128)} %fusion.163, f32[2,64,512,48]{2,3,1,0:T(8,128)} %fusion.164, f32[2,64,512,48]{2,3,1,0:T(8,128)} %fusion.165, f32[2,64,512,48]{2,3,1,0:T(8,128)} %fusion.166, f32[2,64,512,48]{2,3,1,0:T(8,128)} %fusion.167, f32[2,64,512,48]{2,3,1,0:T(8,128)} %fusion.168, ...), kind=kOutput, calls=%fused_computation.13.clone.1 | convolution fusion | flops 497025024 | bytes 111695872 | tf_op jit(solution)/shard_map/while/body/eval_jaxpr/io,inxt->onxt/dot_general | solution.py:52
  312.1 10.1 %select_convert_fusion.5 = bf16[48,2,64,512]{3,0,2,1:T(8,128)(2,1)S(1)} fusion(f32[2,64,512]{2,1,0:T(8,128)S(1)} %get-tuple-element.303, f32[48]{0:T(128)S(1)} %get-tuple-element.304, f32[2,64,512]{2,1,0:T(8,128)S(1)} %get-tuple-element.305, f32[48]{0:T(128)S(1)} %get-tuple-element.306, f32[2,64,512]{2,1,0:T(8,128)S(1)} %get-tuple-element.307, ...), kind=kLoop, calls=%fused_computation.12.clone.3 | loop fusion | flops 72351744 | bytes 8652992 | tf_op jit(solution)/shard_map/while/body/eval_jaxpr/convert_element_type | solution.py:48
  327.8 5.6 fusion.169
  349.9 5.6 fusion.165
  361.1 5.6 fusion.163
  366.7 39.3 %fusion.171 = bf16[48,2,64,512]{3,0,2,1:T(8,128)(2,1)} fusion(f32[2,64,512,48]{2,3,1,0:T(8,128)} %fusion.163, f32[2,64,512,48]{2,3,1,0:T(8,128)} %fusion.164, f32[2,64,512,48]{2,3,1,0:T(8,128)} %fusion.165, f32[2,64,512,48]{2,3,1,0:T(8,128)} %fusion.166, f32[2,64,512,48]{2,3,1,0:T(8,128)} %fusion.167, f32[2,64,512,48]{2,3,1,0:T(8,128)} %fusion.168, ...), kind=kOutput, calls=%fused_computation.13.clone.1 | convolution fusion | flops 497025024 | bytes 111695872 | tf_op jit(solution)/shard_map/while/body/eval_jaxpr/io,inxt->onxt/dot_general | solution.py:52
  432.6 10.1 %select_convert_fusion.5 = bf16[48,2,64,512]{3,0,2,1:T(8,128)(2,1)S(1)} fusion(f32[2,64,512]{2,1,0:T(8,128)S(1)} %get-tuple-element.303, f32[48]{0:T(128)S(1)} %get-tuple-element.304, f32[2,64,512]{2,1,0:T(8,128)S(1)} %get-tuple-element.305, f32[48]{0:T(128)S(1)} %get-tuple-element.306, f32[2,64,512]{2,1,0:T(8,128)S(1)} %get-tuple-element.307, ...), kind=kLoop, calls=%fused_computation.12.clone.3 | loop fusion | flops 72351744 | bytes 8652992 | tf_op jit(solution)/shard_map/while/body/eval_jaxpr/convert_element_type | solution.py:48
  470.4 5.6 fusion.165
  481.6 5.6 fusion.163
  487.2 39.3 %fusion.171 = bf16[48,2,64,512]{3,0,2,1:T(8,128)(2,1)} fusion(f32[2,64,512,48]{2,3,1,0:T(8,128)} %fusion.163, f32[2,64,512,48]{2,3,1,0:T(8,128)} %fusion.164, f32[2,64,512,48]{2,3,1,0:T(8,128)} %fusion.165, f32[2,64,512,48]{2,3,1,0:T(8,128)} %fusion.166, f32[2,64,512,48]{2,3,1,0:T(8,128)} %fusion.167, f32[2,64,512,48]{2,3,1,0:T(8,128)} %fusion.168, ...), kind=kOutput, calls=%fused_computation.13.clone.1 | convolution fusion | flops 497025024 | bytes 111695872 | tf_op jit(solution)/shard_map/while/body/eval_jaxpr/io,inxt->onxt/dot_general | solution.py:52
  553.1 10.1 %select_convert_fusion.5 = bf16[48,2,64,512]{3,0,2,1:T(8,128)(2,1)S(1)} fusion(f32[2,64,512]{2,1,0:T(8,128)S(1)} %get-tuple-element.303, f32[48]{0:T(128)S(1)} %get-tuple-element.304, f32[2,64,512]{2,1,0:T(8,128)S(1)} %get-tuple-element.305, f32[48]{0:T(128)S(1)} %get-tuple-element.306, f32[2,64,512]{2,1,0:T(8,128)S(1)} %get-tuple-element.307, ...), kind=kLoop, calls=%fused_computation.12.clone.3 | loop fusion | flops 72351744 | bytes 8652992 | tf_op jit(solution)/shard_map/while/body/eval_jaxpr/convert_element_type | solution.py:48
  590.9 5.6 fusion.165
  607.7 39.3 %fusion.171 = bf16[48,2,64,512]{3,0,2,1:T(8,128)(2,1)} fusion(f32[2,64,512,48]{2,3,1,0:T(8,128)} %fusion.163, f32[2,64,512,48]{2,3,1,0:T(8,128)} %fusion.164, f32[2,64,512,48]{2,3,1,0:T(8,128)} %fusion.165, f32[2,64,512,48]{2,3,1,0:T(8,128)} %fusion.166, f32[2,64,512,48]{2,3,1,0:T(8,128)} %fusion.167, f32[2,64,512,48]{2,3,1,0:T(8,128)} %fusion.168, ...), kind=kOutput, calls=%fused_computation.13.clone.1 | convolution fusion | flops 497025024 | bytes 111695872 | tf_op jit(solution)/shard_map/while/body/eval_jaxpr/io,inxt->onxt/dot_general | solution.py:52
  745.9 32.3 %psum.7 = f32[]{:T(128)} all-reduce(f32[]{:T(128)} %multiply_reduce_fusion), channel_id=1, replica_groups=mesh['line'=2,'bin'=16] {'bin'}, use_global_device_ids=true, to_apply=%region_7.9 | all-reduce | flops 1 | bytes 8 | tf_op jit(solution)/shard_map/psum | solution.py:132
  (222 shorter events, 391.3 us)
Async XLA Ops:
  2.6 13.7 %all-to-all-start = ((s32[16,1,16]{2,1,0:T(1,128)}), s32[16,1,16]{2,1,0:T(1,128)S(1)}, u32[]{:S(2)}, u32[]{:S(2)}) async-start(s32[16,1,16]{2,1,0:T(1,128)} %all_to_all.9), calls=%async_computation | async-start | bytes 16384 | tf_op jit(solution)/shard_map/all_to_all | solution.py:106
  16.3 26.6 %all-to-all-start.1 = ((bf16[16,16,2048]{2,1,0:T(8,128)(2,1)}), bf16[16,16,2048]{2,1,0:T(8,128)(2,1)S(1)}, u32[]{:S(2)}, u32[]{:S(2)}) async-start(bf16[16,16,2048]{2,1,0:T(8,128)(2,1)} %bitcast.76), calls=%async_computation.1 | async-start | bytes 2097152 | tf_op jit(solution)/shard_map/all_to_all | solution.py:105
  46.9 630.8 %copy-start.3 = (pred[16,16]{1,0:T(8,128)(4,1)S(1)}, pred[16,16]{1,0:T(8,128)(4,1)}, u32[]{:S(2)}) copy-start(pred[16,16]{1,0:T(8,128)(4,1)} %compare_bitcast_fusion) | copy-start | bytes 772
  126.1 39.3 %copy-start.2 = (bf16[3,3,48]{2,1,0:T(4,128)(2,1)S(1)}, bf16[3,3,48]{2,1,0:T(4,128)(2,1)}, u32[]{:S(2)}) copy-start(bf16[3,3,48]{2,1,0:T(4,128)(2,1)} %get-tuple-element.353) | copy-start | bytes 2596 | tf_op jit(solution)/shard_map/while
  246.2 39.3 %copy-start.2 = (bf16[3,3,48]{2,1,0:T(4,128)(2,1)S(1)}, bf16[3,3,48]{2,1,0:T(4,128)(2,1)}, u32[]{:S(2)}) copy-start(bf16[3,3,48]{2,1,0:T(4,128)(2,1)} %get-tuple-element.353) | copy-start | bytes 2596 | tf_op jit(solution)/shard_map/while
  366.7 39.3 %copy-start.2 = (bf16[3,3,48]{2,1,0:T(4,128)(2,1)S(1)}, bf16[3,3,48]{2,1,0:T(4,128)(2,1)}, u32[]{:S(2)}) copy-start(bf16[3,3,48]{2,1,0:T(4,128)(2,1)} %get-tuple-element.353) | copy-start | bytes 2596 | tf_op jit(solution)/shard_map/while
  487.2 39.3 %copy-start.2 = (bf16[3,3,48]{2,1,0:T(4,128)(2,1)S(1)}, bf16[3,3,48]{2,1,0:T(4,128)(2,1)}, u32[]{:S(2)}) copy-start(bf16[3,3,48]{2,1,0:T(4,128)(2,1)} %get-tuple-element.353) | copy-start | bytes 2596 | tf_op jit(solution)/shard_map/while
  607.7 39.3 %copy-start.2 = (bf16[3,3,48]{2,1,0:T(4,128)(2,1)S(1)}, bf16[3,3,48]{2,1,0:T(4,128)(2,1)}, u32[]{:S(2)}) copy-start(bf16[3,3,48]{2,1,0:T(4,128)(2,1)} %get-tuple-element.353) | copy-start | bytes 2596 | tf_op jit(solution)/shard_map/while
  675.0 68.8 %copy-start.1 = (f32[128,2048]{1,0:T(8,128)S(1)}, f32[128,2048]{1,0:T(8,128)}, u32[]{:S(2)}) copy-start(f32[128,2048]{1,0:T(8,128)} %param.14) | copy-start | bytes 3145732
  678.3 7.9 %collective-permute-start = (bf16[1,16,2048]{2,1,0:T(8,128)(2,1)S(1)}, bf16[1,16,2048]{2,1,0:T(8,128)(2,1)S(1)}, u32[]{:S(2)}, u32[]{:S(2)}) collective-permute-start(bf16[1,16,2048]{2,1,0:T(8,128)(2,1)S(1)} %get-tuple-element.240), channel_id=1, source_target_pairs={{0,15},{1,0},{2,1},{3,2},{4,3},{5,4},{6,5},{7,6},{8,7},{9,8},{10,9... | collective-permute-start | bytes 196616 | tf_op jit(solution)/shard_map/ppermute | solution.py:127
  683.7 58.6 %collective-permute-start.14 = (bf16[1,16,2048]{2,1,0:T(8,128)(2,1)S(1)}, bf16[1,16,2048]{2,1,0:T(8,128)(2,1)S(1)}, u32[]{:S(2)}, u32[]{:S(2)}) collective-permute-start(bf16[1,16,2048]{2,1,0:T(8,128)(2,1)S(1)} %get-tuple-element.226), channel_id=1, source_target_pairs={{0,1},{1,2},{2,3},{3,4},{4,5},{5,6},{6,7},{7,8},{8,9},{9,10},{10,1... | collective-permute-start | bytes 196616 | tf_op jit(solution)/shard_map/ppermute | solution.py:127
  683.8 58.6 %collective-permute-start.13 = (bf16[1,16,2048]{2,1,0:T(8,128)(2,1)S(1)}, bf16[1,16,2048]{2,1,0:T(8,128)(2,1)S(1)}, u32[]{:S(2)}, u32[]{:S(2)}) collective-permute-start(bf16[1,16,2048]{2,1,0:T(8,128)(2,1)S(1)} %get-tuple-element.227), channel_id=1, source_target_pairs={{0,2},{1,3},{2,4},{3,5},{4,6},{5,7},{6,8},{7,9},{8,10},{9,11},{10,... | collective-permute-start | bytes 196616 | tf_op jit(solution)/shard_map/ppermute | solution.py:127
  683.9 58.5 %collective-permute-start.12 = (bf16[1,16,2048]{2,1,0:T(8,128)(2,1)S(1)}, bf16[1,16,2048]{2,1,0:T(8,128)(2,1)S(1)}, u32[]{:S(2)}, u32[]{:S(2)}) collective-permute-start(bf16[1,16,2048]{2,1,0:T(8,128)(2,1)S(1)} %get-tuple-element.228), channel_id=1, source_target_pairs={{0,3},{1,4},{2,5},{3,6},{4,7},{5,8},{6,9},{7,10},{8,11},{9,12},{10... | collective-permute-start | bytes 196616 | tf_op jit(solution)/shard_map/ppermute | solution.py:127
  685.0 57.4 %collective-permute-start.11 = (bf16[1,16,2048]{2,1,0:T(8,128)(2,1)S(1)}, bf16[1,16,2048]{2,1,0:T(8,128)(2,1)S(1)}, u32[]{:S(2)}, u32[]{:S(2)}) collective-permute-start(bf16[1,16,2048]{2,1,0:T(8,128)(2,1)S(1)} %get-tuple-element.229), channel_id=1, source_target_pairs={{0,4},{1,5},{2,6},{3,7},{4,8},{5,9},{6,10},{7,11},{8,12},{9,13},{1... | collective-permute-start | bytes 196616 | tf_op jit(solution)/shard_map/ppermute | solution.py:127
  686.3 6.7 collective-permute-start.1
  693.0 3.7 collective-permute-start.2
  696.7 5.0 collective-permute-start.3
  701.7 4.9 collective-permute-start.4
  706.5 6.1 collective-permute-start.5
  712.6 6.1 collective-permute-start.6
  718.7 6.7 collective-permute-start.7
  725.4 4.8 collective-permute-start.8
  730.3 6.6 collective-permute-start.9
  736.8 5.5 collective-permute-start.10
  (7 other events, 72.6 us)
